TPU v7x, 32 devices: a whole 2x2x4 slice. The times are simulated.
32 devices in a mesh: grp: 2 (over y), section: 2 (over core), seq: 4 (over z), fsdp: 2 (over x).
Axes of the slice: x: 2, y: 2, z: 4, core: 2. Of those that a mesh axis runs over, the one named last changes fastest.
Arguments:
- head_inputs: bfloat16 [2, 4, 256, 7680], P('section', ('grp', 'fsdp'), 'seq'), parts along dimension 1, may hold values from -8 to 8
- hidden: bfloat16 [2, 4, 256, 2560], P('section', ('grp', 'fsdp'), 'seq'), parts along dimension 1, may hold values from -3 to 3
- out_weight: bfloat16 [2, 2560, 2560], P('section', 'fsdp'), may hold values from -0.125 to 0.125
- time_weight: bfloat16 [2, 256, 7680], P('section', None, ('seq', 'fsdp')), may hold values from -0.375 to 0.375
- head_weight: bfloat16 [2, 2560, 64], P('section', ('seq', 'fsdp')), may hold values from -0.125 to 0.125
- latent: float32 [2, 4, 128, 128], P('section', ('grp', 'fsdp'), 'seq'), parts along dimension 1, may hold values from -6 to 6
- timesteps: int32 [2, 4, 2], P('section', ('grp', 'fsdp')), parts along dimension 1, may hold values from 41 to 999, as said below
Outputs:
- velocity: float32 [2, 4, 128, 128], P('section', ('grp', 'fsdp'), 'seq'), parts along dimension 1
- carried: float32 [2, 4, 128, 128], P('section', ('grp', 'fsdp'), 'seq'), parts along dimension 1
There are 2 independent parts, one for each index of `grp`. A program takes and returns all parts, laid end to end along the dimension named above; an argument that names none is the same for every part. Nothing has to cross between parts.
Inputs may be any that keep to these rules, and one draw needn't show every extreme that they name: timesteps[0] lie in 875 to 999 and timesteps[1] in 100 to 874 for the current entry; the next entry is the current one minus 10 to 59.
All inputs are finite; a program needn't handle non-finite values.
Results may differ from a plain program's by a relative error of at most 0.0049.
Values may be sent and summed in bfloat16 or wider, within the bound.
No kernel may reach another device: no remote copies, remote signals or barrier semaphores. Data moves between devices by JAX's collectives and lax.ppermute only.
A program may use at most 128 MiB of HBM per device.

v0:
```python
import math
import jax
import jax.numpy as jnp
from jax import lax
from jax.sharding import PartitionSpec as P

DIM = 2560
HEADS = 32
HEAD = 80
PATCH = 64
FREQ = 256


def partner(block, axis, apart):
    count = lax.axis_size(axis)
    route = []
    for low in range(count):
        high = low | 1 << apart
        if high != low and high < count:
            route += [(low, high), (high, low)]
    return lax.ppermute(block, axis, route)


def time_embed(steps_now):
    half = FREQ // 2
    freqs = jnp.exp(-math.log(10000.0) * jnp.arange(half, dtype=jnp.float32) / half)
    angle = steps_now.astype(jnp.float32)[..., None] * freqs
    return jnp.concatenate([jnp.cos(angle), jnp.sin(angle)], axis=-1)


def sigma_of(steps_now):
    unit_time = steps_now.astype(jnp.float32) / 1000.0
    return 5.0 * unit_time / (1.0 + 4.0 * unit_time)


def attend(exchanged):
    items = exchanged.shape[0]
    length = exchanged.shape[1]
    local_heads = exchanged.shape[2]
    query_all = exchanged[..., :HEAD]
    key_rows = exchanged[..., HEAD : 2 * HEAD]
    value_rows = exchanged[..., 2 * HEAD :]
    block_rows = min(512, length)
    block_count = length // block_rows

    def one_block(block_index):
        query_block = lax.dynamic_slice_in_dim(query_all, block_index * block_rows, block_rows, 1)
        scores = jnp.einsum(
            "nqhe,nkhe->nhqk", query_block, key_rows, preferred_element_type=jnp.float32
        ) * HEAD ** (-0.5)
        row_max = jnp.max(scores, axis=-1, keepdims=True)
        exp_scores = jnp.exp(scores - row_max)
        row_sum = jnp.sum(exp_scores, axis=-1, keepdims=True)
        weights = (exp_scores / row_sum).astype(jnp.bfloat16)
        return jnp.einsum(
            "nhqk,nkhe->nqhe", weights, value_rows, preferred_element_type=jnp.float32
        ).astype(jnp.bfloat16)

    blocks = lax.map(one_block, jnp.arange(block_count, dtype=jnp.int32))
    return blocks.transpose(1, 0, 2, 3, 4).reshape(items, length, local_heads * HEAD)


def body(head_inputs, hidden, out_weight, time_weight, head_weight, latent, timesteps):
    samples = head_inputs.shape[1]
    row_count = head_inputs.shape[2]
    flat_count = samples * row_count
    local = head_inputs.reshape(samples, row_count, HEADS, 3 * HEAD)
    attended = lax.all_to_all(
        attend(lax.all_to_all(local, "seq", split_axis=2, concat_axis=1, tiled=True)),
        "seq",
        split_axis=1,
        concat_axis=2,
        tiled=True,
    )
    flattened = attended.reshape(flat_count, HEADS * HEAD)
    time_full, head_full = (
        lax.all_gather(time_weight, ("seq", "fsdp"), axis=2, tiled=True),
        lax.all_gather(head_weight, ("seq", "fsdp"), axis=1, tiled=True),
    )
    embedding = time_embed(timesteps[0, :, 0]).astype(jnp.bfloat16)
    modulation = jnp.dot(embedding, time_full[0], preferred_element_type=jnp.float32)
    gate_term = modulation[:, None, :DIM]
    shift_term = modulation[:, None, DIM : 2 * DIM]
    scale_term = modulation[:, None, 2 * DIM :]
    own_columns = lax.all_to_all(flattened, "fsdp", split_axis=1, concat_axis=0, tiled=True)
    projected = lax.psum_scatter(
        jnp.dot(own_columns, out_weight[0], preferred_element_type=jnp.float32).astype(
            jnp.bfloat16
        ),
        "fsdp",
        scatter_dimension=0,
        tiled=True,
    ).astype(jnp.float32)
    updated = hidden.reshape(samples, row_count, DIM).astype(
        jnp.float32
    ) + gate_term * projected.reshape(samples, row_count, DIM)
    average = jnp.mean(updated, axis=-1, keepdims=True)
    centred = updated - average
    variance = jnp.mean(centred * centred, axis=-1, keepdims=True)
    normed = (centred * lax.rsqrt(variance + 1e-06) * (1.0 + scale_term) + shift_term).astype(
        jnp.bfloat16
    )
    velocity = jnp.dot(
        normed.reshape(flat_count, DIM), head_full[0], preferred_element_type=jnp.float32
    )
    velocity = velocity.reshape(1, samples, row_count // 2, 2 * PATCH)
    step_size = sigma_of(timesteps[0, :, 1]) - sigma_of(timesteps[0, :, 0])
    stepped = latent + step_size[None, :, None, None] * velocity
    carried = partner(stepped, "section", 0)
    return (velocity, carried)


def solution(mesh):
    return jax.shard_map(
        body,
        mesh=mesh,
        in_specs=(
            P("section", ("grp", "fsdp"), "seq", None),
            P("section", ("grp", "fsdp"), "seq", None),
            P("section", "fsdp", None),
            P("section", None, ("seq", "fsdp")),
            P("section", ("seq", "fsdp"), None),
            P("section", ("grp", "fsdp"), "seq", None),
            P("section", ("grp", "fsdp"), None),
        ),
        out_specs=(
            P("section", ("grp", "fsdp"), "seq", None),
            P("section", ("grp", "fsdp"), "seq", None),
        ),
        check_vma=False,
    )
```

profile of v0, /device:TPU:0, one launch (start us, length us, event | category | flops | bytes accessed | tf_op | source)
XLA Modules:
  0.0 163.8 jit_solution(13938546322388415020)
XLA Ops:
  8.0 0.0 all-gather.2.cloned.1.call-start
  8.0 0.7 all-gather.2.cloned.1.call-update
  8.7 0.0 reduce-scatter.2.cloned.1.call-start
  8.8 3.5 %reshape.152 = bf16[1,64,32,240]{3,2,1,0:T(8,128)(2,1)S(1)} reshape(bf16[1,1,64,7680]{3,2,1,0:T(8,128)(2,1)} %param.7) | data formatting | bytes 1966080 | tf_op jit(solution)/shard_map/reshape | solution.py:67
  12.3 0.6 copy.28
  12.9 47.7 %all_to_all.52 = bf16[1,64,32,240]{3,1,0,2:T(8,128)(2,1)S(1)} all-to-all(bf16[1,64,32,240]{3,1,0,2:T(8,128)(2,1)S(1)} %copy.28), channel_id=1, replica_groups=mesh['grp'=2,'section'=2,'seq'=4,'fsdp'=2] {'seq'}, dimensions={2} | all-to-all | bytes 1966080 | tf_op jit(solution)/shard_map/all_to_all | solution.py:69
  60.6 0.6 copy.46
  61.2 0.1 copy.30
  61.2 0.4 fusion.35
  61.7 0.3 copy.42
  62.0 0.3 copy.43
  62.3 0.3 copy.44
  62.7 2.2 %fusion.37 = (f32[8,256]{1,0:T(8,128)S(1)}, f32[8,256,256]{1,2,0:T(8,128)}) fusion(bf16[1,256,8,80]{1,3,2,0:T(8,128)(2,1)S(1)} %copy.44, bf16[1,256,8,80]{1,3,2,0:T(8,128)(2,1)S(1)} %copy.43), kind=kOutput, calls=%fused_computation.41 | convolution fusion | flops 85459200 | bytes 2760704 | tf_op jit(solution)/shard_map/while/body/eval_jaxpr/sub | solution.py:52
  64.8 1.9 %convolution_convert_fusion = bf16[8,256,80]{1,2,0:T(8,128)(2,1)S(1)} fusion(f32[8,256,256]{1,2,0:T(8,128)} %get-tuple-element.26, f32[8,256]{1,0:T(8,128)S(1)} %get-tuple-element.25, bf16[1,256,8,80]{1,3,2,0:T(8,128)(2,1)S(1)} %copy.42), kind=kOutput, calls=%fused_computation.10 | convolution fusion | flops 85098496 | bytes 2760704 | tf_op jit(solution)/shard_map/while/body/eval_jaxpr/nhqk,nkhe->nqhe/dot_general | solution.py:55
  66.7 0.6 copy.35
  67.3 0.5 broadcast.88
  67.9 2.6 %reduce.14 = bf16[256,640]{1,0:T(8,128)(2,1)S(1)} reduce(bf16[256,1,640]{2,1,0:T(2,128)(2,1)S(1)} %bitcast.71, bf16[]{:T(256)} %broadcast.88), dimensions={1}, to_apply=%bitcast.60.reduce_sub_computation | reduce | bytes 655362
  70.5 0.1 reshape.166
  70.6 22.7 %all_to_all.53 = bf16[4,2,20480]{2,1,0:T(2,128)(2,1)S(1)} all-to-all(bf16[4,2,20480]{2,1,0:T(2,128)(2,1)S(1)} %reshape.166), channel_id=1, replica_groups=mesh['grp'=2,'section'=2,'seq'=4,'fsdp'=2] {'seq'}, dimensions={0} | all-to-all | bytes 655360 | tf_op jit(solution)/shard_map/all_to_all | solution.py:68
  93.2 0.3 reshape.167
  93.6 0.3 copy.36
  93.9 0.2 all_to_all.45
  94.1 8.1 %all_to_all.54 = bf16[64,2,1280]{2,0,1:T(8,128)(2,1)S(1)} all-to-all(bf16[64,2,1280]{2,0,1:T(8,128)(2,1)S(1)} %copy.37), channel_id=1, replica_groups=mesh['grp'=2,'section'=2,'seq'=4,'fsdp'=2] {'fsdp'}, dimensions={1} | all-to-all | bytes 655360 | tf_op jit(solution)/shard_map/all_to_all | solution.py:85
  102.2 0.0 copy-start.4
  102.2 0.0 copy-start.2
  102.2 4.7 %fusion.5 = bf16[128,2560]{1,0:T(8,128)(2,1)} fusion(bf16[128,1280]{1,0:T(8,128)(2,1)S(1)} %bitcast.73, bf16[1,1280,2560]{2,1,0:T(8,128)(2,1)} %param.9), kind=kOutput, calls=%fused_computation.5 | convolution fusion | flops 839188480 | bytes 7536640 | tf_op jit(solution)/shard_map/dot_general | solution.py:87
  106.9 0.0 reduce-scatter.2.cloned.1.call-update
  106.9 0.0 copy-done.4
  107.0 0.6 fusion.36
  108.8 0.1 sine_convert_fusion
  108.9 0.0 copy-done.2
  108.9 0.2 copy.38
  109.1 37.3 %all_gather.7 = bf16[1,2560,64]{2,0,1:T(2,128)(2,1)S(1)} all-gather(bf16[1,320,64]{2,0,1:T(2,128)(2,1)S(1)} %copy.38), channel_id=1, replica_groups=mesh['grp'=2,'section'=2,'seq'=4,'fsdp'=2] {'seq','fsdp'}, dimensions={1}, use_global_device_ids=true | all-gather | bytes 368640 | tf_op jit(solution)/shard_map/all_gather | solution.py:78
  146.4 0.8 copy.39
  147.1 0.0 copy-start
  147.2 0.0 all-gather.2.cloned.1.call-done
  147.3 3.2 %fusion.3 = f32[1,7680]{1,0:T(1,128)S(1)} fusion(bf16[256,1]{0,1:T(2,128)(2,1)S(1)} %reshape.160, bf16[1,256,7680]{1,2,0:T(8,128)(2,1)} %all-gather.2.cloned.1.call-done), kind=kOutput, calls=%fused_computation.3 | convolution fusion | flops 3932160 | bytes 3963392 | tf_op jit(solution)/shard_map/dot_general | solution.py:81
  150.5 0.0 copy-start.3
  150.5 0.1 slice_reduce_fusion.1
  150.6 0.0 reduce-scatter.2.cloned.1.call-done
  150.6 0.0 copy-done
  150.6 1.2 fusion.10
  151.8 1.2 multiply_reduce_fusion.1
  153.1 1.3 fusion.11
  154.4 0.1 reshape.156
  154.5 0.0 copy-start.1
  154.5 0.0 copy-done.3
  154.5 0.1 collective-permute-start
  154.6 1.2 collective-permute-done
  155.7 0.6 copy.48
  156.3 0.0 copy-done.1
  (7 shorter events, 0.1 us)
Async XLA Ops:
  8.0 139.3 %all-gather.2.cloned.1.call-start = ((), (), s32[]{:S(2)}) async-start(), calls=%async_computation.4 | async-start | bytes 4423680 | tf_op jit(solution)/shard_map/all_gather | solution.py:77
  8.7 141.9 %reduce-scatter.2.cloned.1.call-start = ((), (), s32[]{:S(2)}) async-start(), calls=%async_computation.5 | async-start | bytes 983040 | tf_op jit(solution)/shard_map/reduce_scatter | solution.py:86
  102.2 4.8 %copy-start.4 = (s32[1,1,2]{2,1,0:T(1,128)S(1)}, s32[1,1,2]{2,1,0:T(1,128)}, u32[]{:S(2)}) copy-start(s32[1,1,2]{2,1,0:T(1,128)} %param.13) | copy-start | bytes 28
  102.2 6.7 %copy-start.2 = (bf16[1,320,64]{1,2,0:T(8,128)(2,1)S(1)}, bf16[1,320,64]{1,2,0:T(8,128)(2,1)}, u32[]{:S(2)}) copy-start(bf16[1,320,64]{1,2,0:T(8,128)(2,1)} %param.11) | copy-start | bytes 122884
  147.1 3.5 %copy-start = (bf16[1,1,64,2560]{3,2,1,0:T(8,128)(2,1)S(1)}, bf16[1,1,64,2560]{3,2,1,0:T(8,128)(2,1)}, u32[]{:S(2)}) copy-start(bf16[1,1,64,2560]{3,2,1,0:T(8,128)(2,1)} %param.8) | copy-start | bytes 983044
  150.5 4.0 %copy-start.3 = (f32[1,1,32,128]{3,2,1,0:T(8,128)S(1)}, f32[1,1,32,128]{3,2,1,0:T(8,128)}, u32[]{:S(2)}) copy-start(f32[1,1,32,128]{3,2,1,0:T(8,128)} %param.12) | copy-start | bytes 49156
  154.5 1.9 %copy-start.1 = (f32[1,1,32,128]{3,2,1,0:T(8,128)}, f32[1,1,32,128]{3,2,1,0:T(8,128)S(1)}, u32[]{:S(2)}) copy-start(f32[1,1,32,128]{3,2,1,0:T(8,128)S(1)} %reshape.156) | copy-start | bytes 49156
  154.5 1.2 collective-permute-start
Sparse Core Ops, SparseCore 0:
  11.0 94.3 all-gather.1
Sparse Core Ops, SparseCore 1:
  107.0 29.8 reduce-scatter.1
where the time goes:
time: 164 us
  blocking collectives  116 us (71%)
  between operations  17.1 us (10%)
  matrix products  13.4 us (8%)
  local copies, waits for them, and re-layouts  10.4 us (6%)
  other arithmetic  5.18 us (3%)
  waiting for transfers between devices  1.92 us (1%)
    all_to_all x1, blocking collectives, body(): lax.all_to_all(local, 'seq', split_axis=2, concat_axis=1, tiled=True)  47.7 us
    all_gather x1, blocking collectives, body(): lax.all_gather(head_weight, ('seq', 'fsdp'), axis=1, tiled=True)  37.3 us
    all_to_all x1, blocking collectives, body(): lax.all_to_all(attend(lax.all_to_all(local, 'seq', split_axis=2, concat_a...  22.7 us
    all_to_all x1, blocking collectives, body(): lax.all_to_all(flattened, 'fsdp', split_axis=1, concat_axis=0, tiled=True)  8.07 us
    dot_general x1, matrix products, body(): jnp.dot(own_columns, out_weight[0], preferred_element_type=jnp.float32)  4.74 us
    reshape x2, local copies, waits for them, and re-layouts, body(): local = head_inputs.reshape(samples, row_count, HEADS, 3 * HEAD)  4.12 us
  transfers between devices with their start and end apart: 3, of which 1 were waited for; matrix products, arithmetic and copies ran while one was open for 15% of the time, Pallas kernels for 0%

commit v1 on v0

--- a/solution.py
+++ b/solution.py
@@ -9,6 +9,12 @@
 HEAD = 80
 PATCH = 64
 FREQ = 256
+
+
+def stack_and_merge(shard, mesh_axis, d):
+    pieces = lax.all_gather(shard, mesh_axis, axis=0, tiled=False)
+    out = jnp.concatenate(pieces, axis=d)
+    return out
 
 
 def partner(block, axis, apart):
@@ -75,7 +81,7 @@
     flattened = attended.reshape(flat_count, HEADS * HEAD)
     time_full, head_full = (
         lax.all_gather(time_weight, ("seq", "fsdp"), axis=2, tiled=True),
-        lax.all_gather(head_weight, ("seq", "fsdp"), axis=1, tiled=True),
+        stack_and_merge(head_weight, ("seq", "fsdp"), 1),
     )
     embedding = time_embed(timesteps[0, :, 0]).astype(jnp.bfloat16)
     modulation = jnp.dot(embedding, time_full[0], preferred_element_type=jnp.float32)

time: 164 us -> 158 us (0.963)
  blocking collectives: 116 us -> 110 us
    all_gather x1, blocking collectives: 37.3 us -> 31.4 us  [stack_and_merge(): pieces = lax.all_gather(shard, mesh_axis, axis=0, tiled=False)]
where the time goes in v1:
time: 158 us
  blocking collectives  110 us (70%)
  between operations  17.1 us (11%)
  matrix products  13.4 us (8%)
  local copies, waits for them, and re-layouts  10 us (6%)
  other arithmetic  5.18 us (3%)
  waiting for transfers between devices  1.92 us (1%)
    all_to_all x1, blocking collectives, body(): lax.all_to_all(local, 'seq', split_axis=2, concat_axis=1, tiled=True)  47.7 us
    all_gather x1, blocking collectives, stack_and_merge(): pieces = lax.all_gather(shard, mesh_axis, axis=0, tiled=False)  31.4 us
    all_to_all x1, blocking collectives, body(): lax.all_to_all(attend(lax.all_to_all(local, 'seq', split_axis=2, concat_a...  22.7 us
    all_to_all x1, blocking collectives, body(): lax.all_to_all(flattened, 'fsdp', split_axis=1, concat_axis=0, tiled=True)  8.07 us
    dot_general x1, matrix products, body(): jnp.dot(own_columns, out_weight[0], preferred_element_type=jnp.float32)  4.74 us
    reshape x2, local copies, waits for them, and re-layouts, body(): local = head_inputs.reshape(samples, row_count, HEADS, 3 * HEAD)  4.12 us
    dot_general x1, matrix products, body(): jnp.dot(embedding, time_full[0], preferred_element_type=jnp.float32)  3.22 us
  transfers between devices with their start and end apart: 3, of which 1 were waited for; matrix products, arithmetic and copies ran while one was open for 15% of the time, Pallas kernels for 0%

profile of v1, /device:TPU:0, one launch (start us, length us, event | category | flops | bytes accessed | tf_op | source)
XLA Modules:
  0.0 157.5 jit_solution(7981841623644300827)
XLA Ops:
  8.0 0.0 all-gather.3.cloned.1.call-start
  8.0 0.7 all-gather.3.cloned.1.call-update
  8.7 0.0 reduce-scatter.2.cloned.1.call-start
  8.8 3.5 %reshape.152 = bf16[1,64,32,240]{3,2,1,0:T(8,128)(2,1)S(1)} reshape(bf16[1,1,64,7680]{3,2,1,0:T(8,128)(2,1)} %param.7) | data formatting | bytes 1966080 | tf_op jit(solution)/shard_map/reshape | solution.py:73
  12.3 0.6 copy.29
  12.9 47.7 %all_to_all.52 = bf16[1,64,32,240]{3,1,0,2:T(8,128)(2,1)S(1)} all-to-all(bf16[1,64,32,240]{3,1,0,2:T(8,128)(2,1)S(1)} %copy.29), channel_id=1, replica_groups=mesh['grp'=2,'section'=2,'seq'=4,'fsdp'=2] {'seq'}, dimensions={2} | all-to-all | bytes 1966080 | tf_op jit(solution)/shard_map/all_to_all | solution.py:75
  60.6 0.6 copy.46
  61.2 0.1 copy.31
  61.2 0.4 fusion.30
  61.7 0.3 copy.42
  62.0 0.3 copy.43
  62.3 0.3 copy.44
  62.7 2.2 %fusion.32 = (f32[8,256]{1,0:T(8,128)S(1)}, f32[8,256,256]{1,2,0:T(8,128)}) fusion(bf16[1,256,8,80]{1,3,2,0:T(8,128)(2,1)S(1)} %copy.44, bf16[1,256,8,80]{1,3,2,0:T(8,128)(2,1)S(1)} %copy.43), kind=kOutput, calls=%fused_computation.36 | convolution fusion | flops 85459200 | bytes 2760704 | tf_op jit(solution)/shard_map/while/body/eval_jaxpr/sub | solution.py:58
  64.8 1.9 %convolution_convert_fusion = bf16[8,256,80]{1,2,0:T(8,128)(2,1)S(1)} fusion(f32[8,256,256]{1,2,0:T(8,128)} %get-tuple-element.26, f32[8,256]{1,0:T(8,128)S(1)} %get-tuple-element.25, bf16[1,256,8,80]{1,3,2,0:T(8,128)(2,1)S(1)} %copy.42), kind=kOutput, calls=%fused_computation.10 | convolution fusion | flops 85098496 | bytes 2760704 | tf_op jit(solution)/shard_map/while/body/eval_jaxpr/nhqk,nkhe->nqhe/dot_general | solution.py:61
  66.7 0.6 copy.36
  67.3 0.5 broadcast.88
  67.9 2.6 %reduce.14 = bf16[256,640]{1,0:T(8,128)(2,1)S(1)} reduce(bf16[256,1,640]{2,1,0:T(2,128)(2,1)S(1)} %bitcast.71, bf16[]{:T(256)} %broadcast.88), dimensions={1}, to_apply=%bitcast.59.reduce_sub_computation | reduce | bytes 655362
  70.5 0.1 reshape.168
  70.6 22.7 %all_to_all.53 = bf16[4,2,20480]{2,1,0:T(2,128)(2,1)S(1)} all-to-all(bf16[4,2,20480]{2,1,0:T(2,128)(2,1)S(1)} %reshape.168), channel_id=1, replica_groups=mesh['grp'=2,'section'=2,'seq'=4,'fsdp'=2] {'seq'}, dimensions={0} | all-to-all | bytes 655360 | tf_op jit(solution)/shard_map/all_to_all | solution.py:74
  93.2 0.3 reshape.169
  93.6 0.3 copy.37
  93.9 0.2 all_to_all.45
  94.1 8.1 %all_to_all.54 = bf16[64,2,1280]{2,0,1:T(8,128)(2,1)S(1)} all-to-all(bf16[64,2,1280]{2,0,1:T(8,128)(2,1)S(1)} %copy.38), channel_id=1, replica_groups=mesh['grp'=2,'section'=2,'seq'=4,'fsdp'=2] {'fsdp'}, dimensions={1} | all-to-all | bytes 655360 | tf_op jit(solution)/shard_map/all_to_all | solution.py:91
  102.2 0.0 copy-start.4
  102.2 0.0 copy-start.2
  102.2 4.7 %fusion.5 = bf16[128,2560]{1,0:T(8,128)(2,1)} fusion(bf16[128,1280]{1,0:T(8,128)(2,1)S(1)} %bitcast.73, bf16[1,1280,2560]{2,1,0:T(8,128)(2,1)} %param.9), kind=kOutput, calls=%fused_computation.5 | convolution fusion | flops 839188480 | bytes 7536640 | tf_op jit(solution)/shard_map/dot_general | solution.py:93
  106.9 0.0 reduce-scatter.2.cloned.1.call-update
  106.9 0.0 copy-done.4
  107.0 0.6 fusion.31
  108.8 0.1 sine_convert_fusion
  108.9 0.0 copy-done.2
  108.9 31.4 %all-gather = bf16[8,320,64]{1,2,0:T(8,128)(2,1)S(1)} all-gather(bf16[1,320,64]{1,2,0:T(8,128)(2,1)S(1)} %copy-done.2), channel_id=2, replica_groups=mesh['grp'=2,'section'=2,'seq'=4,'fsdp'=2] {'seq','fsdp'}, dimensions={0}, use_global_device_ids=true | all-gather | bytes 368640 | tf_op jit(solution)/shard_map/all_gather | solution.py:15
  140.4 0.2 copy.39
  140.6 0.3 squeeze_reshape.3
  140.9 0.0 copy-start
  141.0 0.0 all-gather.3.cloned.1.call-done
  141.0 3.2 %fusion.3 = f32[1,7680]{1,0:T(1,128)S(1)} fusion(bf16[256,1]{0,1:T(2,128)(2,1)S(1)} %reshape.162, bf16[1,256,7680]{1,2,0:T(8,128)(2,1)} %all-gather.3.cloned.1.call-done), kind=kOutput, calls=%fused_computation.3 | convolution fusion | flops 3932160 | bytes 3963392 | tf_op jit(solution)/shard_map/dot_general | solution.py:87
  144.2 0.0 copy-start.3
  144.2 0.1 slice_reduce_fusion.1
  144.3 0.0 reduce-scatter.2.cloned.1.call-done
  144.4 0.0 copy-done
  144.4 1.2 fusion.10
  145.6 1.2 multiply_reduce_fusion.1
  146.8 1.3 fusion.15
  148.1 0.1 reshape.156
  148.2 0.0 copy-start.1
  148.2 0.0 copy-done.3
  148.2 0.1 collective-permute-start
  148.3 1.2 collective-permute-done
  149.5 0.6 copy.48
  150.1 0.0 copy-done.1
  (7 shorter events, 0.1 us)
Async XLA Ops:
  8.0 133.0 %all-gather.3.cloned.1.call-start = ((), (), s32[]{:S(2)}) async-start(), calls=%async_computation.4 | async-start | bytes 4423680 | tf_op jit(solution)/shard_map/all_gather | solution.py:83
  8.7 135.6 %reduce-scatter.2.cloned.1.call-start = ((), (), s32[]{:S(2)}) async-start(), calls=%async_computation.5 | async-start | bytes 983040 | tf_op jit(solution)/shard_map/reduce_scatter | solution.py:92
  102.2 4.8 %copy-start.4 = (s32[1,1,2]{2,1,0:T(1,128)S(1)}, s32[1,1,2]{2,1,0:T(1,128)}, u32[]{:S(2)}) copy-start(s32[1,1,2]{2,1,0:T(1,128)} %param.13) | copy-start | bytes 28
  102.2 6.7 %copy-start.2 = (bf16[1,320,64]{1,2,0:T(8,128)(2,1)S(1)}, bf16[1,320,64]{1,2,0:T(8,128)(2,1)}, u32[]{:S(2)}) copy-start(bf16[1,320,64]{1,2,0:T(8,128)(2,1)} %param.11) | copy-start | bytes 122884
  140.9 3.5 %copy-start = (bf16[1,1,64,2560]{3,2,1,0:T(8,128)(2,1)S(1)}, bf16[1,1,64,2560]{3,2,1,0:T(8,128)(2,1)}, u32[]{:S(2)}) copy-start(bf16[1,1,64,2560]{3,2,1,0:T(8,128)(2,1)} %param.8) | copy-start | bytes 983044
  144.2 4.0 %copy-start.3 = (f32[1,1,32,128]{3,2,1,0:T(8,128)S(1)}, f32[1,1,32,128]{3,2,1,0:T(8,128)}, u32[]{:S(2)}) copy-start(f32[1,1,32,128]{3,2,1,0:T(8,128)} %param.12) | copy-start | bytes 49156
  148.2 1.9 %copy-start.1 = (f32[1,1,32,128]{3,2,1,0:T(8,128)}, f32[1,1,32,128]{3,2,1,0:T(8,128)S(1)}, u32[]{:S(2)}) copy-start(f32[1,1,32,128]{3,2,1,0:T(8,128)S(1)} %reshape.156) | copy-start | bytes 49156
  148.2 1.2 collective-permute-start
Sparse Core Ops, SparseCore 0:
  11.0 94.3 all-gather.2
Sparse Core Ops, SparseCore 1:
  107.0 17.1 reduce-scatter.1
